TPU v7x, 32 devices: a whole 2x2x4 slice. The times are simulated.
32 devices in a mesh: wide: 16 (over z, y, x), narrow: 2 (over core).
Axes of the slice: x: 2, y: 2, z: 4, core: 2. Of those that a mesh axis runs over, the one named last changes fastest.
Arguments:
- grads: bfloat16 [14, 512, 2048], P(None, 'wide', 'narrow'), may hold values from -200 to 200
- momentum: float32 [14, 512, 2048], P(None, 'wide', 'narrow'), may hold values from -400 to 400
- owners: int32 [14], replicated, may hold values from 0 to 15, as said below
- norm_grads: float32 [28, 2048], P('narrow', 'wide'), may hold values from -6 to 6
- norm_params: float32 [28, 2048], P('narrow', 'wide'), may hold values from 0.5 to 1.5
- adam_m: float32 [28, 2048], P('narrow', 'wide'), may hold values from -4 to 4
- adam_v: float32 [28, 2048], P('narrow', 'wide'), may hold values from 0.1 to 4
Outputs:
- muon_update: bfloat16 [14, 512, 2048], P(None, 'wide', 'narrow')
- momentum_new: float32 [14, 512, 2048], P(None, 'wide', 'narrow')
- owner_load: float32 [16], P('wide')
- norm_params_new: float32 [28, 2048], P('narrow', 'wide')
- adam_m_new: float32 [28, 2048], P('narrow', 'wide')
- adam_v_new: float32 [28, 2048], P('narrow', 'wide')
Inputs may be any that keep to these rules, and one draw needn't show every extreme that they name: `owners`: each of the 16 groups owns at most 2 matrices, and some group owns exactly 2.
All inputs are finite; a program needn't handle non-finite values.
Results may differ from a plain program's by a relative error of at most 0.014.
Values may be sent and summed in bfloat16 or wider, within the bound.
A program may use at most 64 MiB of HBM per device.

v0:
```python
import math
import jax
import jax.numpy as jnp
from jax import lax
from jax.sharding import PartitionSpec as P

D = 2048
KV_OUT = 512
ITERS = 2
coef_a = 3.4445
coef_b = -4.775
coef_c = 2.0315
muon_beta = 0.95
norm_eps = 1e-07
adam_first = 0.9
adam_second = 0.95
adam_rate = 0.02
adam_eps = 1e-08
first_fix = 1.0 - 0.9**10
second_fix = 1.0 - 0.95**10


def polynomial_times(current, partial_value):
    gram_sum = lax.psum(partial_value.astype(jnp.bfloat16), "narrow")
    square = jnp.einsum("cmk,ckn->cmn", gram_sum, gram_sum, preferred_element_type=jnp.float32)
    polynomial = (coef_b * gram_sum.astype(jnp.float32) + coef_c * square).astype(jnp.bfloat16)
    return jnp.einsum("cmk,ckn->cmn", polynomial, current, preferred_element_type=jnp.float32)


def newton_schulz(current):
    result = current.astype(jnp.float32)
    for iteration in range(ITERS):
        partial_value = jnp.einsum(
            "cmk,cnk->cmn", current, current, preferred_element_type=jnp.float32
        )
        product_bx = polynomial_times(current, partial_value)
        result = coef_a * current.astype(jnp.float32) + product_bx
        if iteration + 1 < ITERS:
            current = result.astype(jnp.bfloat16)
    updates = (math.sqrt(D) * result).astype(jnp.bfloat16)
    update_values = updates.astype(jnp.float32)
    update_squares = lax.psum(jnp.sum(update_values * update_values, axis=(1, 2)), "narrow")
    return (updates[None], (update_squares / (KV_OUT * D))[None])


def orthogonalize(slot_block):
    directions = slot_block[0]
    square_sums = lax.psum(jnp.sum(directions * directions, axis=(1, 2)), "narrow")
    current = (directions / (jnp.sqrt(square_sums)[:, None, None] + norm_eps)).astype(jnp.bfloat16)
    return newton_schulz(current)


def on_device(grads, momentum, owners, norm_grads, norm_params, adam_m, adam_v):
    grad_values = grads.astype(jnp.float32)
    momentum_new = muon_beta * momentum + grad_values
    direction = grad_values + muon_beta * momentum_new
    groups = lax.axis_size("wide")
    matrix_count = owners.shape[0]
    matrix_ids = jnp.arange(matrix_count, dtype=jnp.int32)
    capacity = -(-matrix_count // groups)
    slot_of = matrix_ids % groups * capacity + matrix_ids // groups
    slot_total = groups * capacity
    slot_match = slot_of[None, :] == jnp.arange(slot_total, dtype=jnp.int32)[:, None]
    source = jnp.sum(jnp.where(slot_match, matrix_ids[None, :], 0), axis=1) + jnp.where(
        jnp.any(slot_match, axis=1), 0, matrix_count
    )
    row_count = direction.shape[1]
    col_count = direction.shape[2]
    padded = jnp.concatenate([direction, jnp.zeros((1, row_count, col_count), jnp.float32)], axis=0)
    outgoing = jnp.take(padded, source, axis=0).reshape(groups, capacity, row_count, col_count)
    updates, slot_loads = orthogonalize(
        lax.all_to_all(outgoing, "wide", split_axis=0, concat_axis=2, tiled=True)
    )
    returned = lax.all_to_all(updates, "wide", split_axis=2, concat_axis=0, tiled=True)
    arrived = returned.reshape(slot_total, row_count, col_count)
    muon_update = jnp.take(arrived, slot_of, axis=0)
    own_group = lax.axis_index("wide")
    computed_here = matrix_ids % groups == own_group
    local_loads = jnp.where(computed_here, jnp.take(slot_loads[0], matrix_ids // groups), 0.0)
    matrix_loads = lax.psum(local_loads, "wide")
    owner_load = jnp.sum(jnp.where(owners == own_group, matrix_loads, 0.0)).reshape(1)
    adam_m_new = adam_first * adam_m + (1.0 - adam_first) * norm_grads
    adam_v_new = adam_second * adam_v + (1.0 - adam_second) * norm_grads * norm_grads
    corrected = adam_m_new / first_fix / (jnp.sqrt(adam_v_new / second_fix) + adam_eps)
    norm_params_new = norm_params - adam_rate * corrected
    return (muon_update, momentum_new, owner_load, norm_params_new, adam_m_new, adam_v_new)


def solution(mesh):
    return jax.shard_map(
        on_device,
        mesh=mesh,
        in_specs=(
            P(None, "wide", "narrow"),
            P(None, "wide", "narrow"),
            P(),
            P("narrow", "wide"),
            P("narrow", "wide"),
            P("narrow", "wide"),
            P("narrow", "wide"),
        ),
        out_specs=(
            P(None, "wide", "narrow"),
            P(None, "wide", "narrow"),
            P("wide"),
            P("narrow", "wide"),
            P("narrow", "wide"),
            P("narrow", "wide"),
        ),
        check_vma=False,
    )
```

profile of v0, /device:TPU:0, one launch (start us, length us, event | category | flops | bytes accessed | tf_op | source)
XLA Modules:
  0.0 207.1 jit_solution(12475647661025235217)
XLA Ops:
  7.2 0.0 all-reduce.4.cloned.1.call-start
  7.2 0.1 fusion.20
  7.3 0.1 select_reduce_fusion
  7.5 3.5 %convert_add_fusion = (f32[14,32,1024]{2,1,0:T(8,128)S(1)}, f32[14,32,1024]{2,1,0:T(8,128)}) fusion(bf16[14,32,1024]{2,1,0:T(8,128)(2,1)} %param.7, f32[14,32,1024]{2,1,0:T(8,128)} %param.8), kind=kLoop, calls=%fused_computation.2 | loop fusion | flops 2293760 | bytes 6422528 | tf_op jit(solution)/shard_map/add | solution.py:56
  11.0 0.3 concatenate.3
  11.2 2.0 gather_fusion
  13.3 1.8 bitcast_select_fusion
  15.1 57.0 %all_to_all.8 = f32[16,1,32,1024]{3,2,1,0:T(8,128)S(1)} all-to-all(f32[16,1,32,1024]{3,2,1,0:T(8,128)S(1)} %bitcast_select_fusion), channel_id=1, replica_groups=mesh['wide'=16,'narrow'=2] {'wide'}, dimensions={0} | all-to-all | bytes 4194304 | tf_op jit(solution)/shard_map/all_to_all | solution.py:72
  72.1 1.1 multiply_reduce_fusion.1
  73.2 3.1 %psum.35 = f32[1]{0:T(128)} all-reduce(f32[1]{0:T(128)} %bitcast.3), channel_id=1, replica_groups=mesh['wide'=16,'narrow'=2] {'narrow'}, use_global_device_ids=true, to_apply=%region_3.4 | all-reduce | flops 1 | bytes 8 | tf_op jit(solution)/shard_map/psum | solution.py:48
  77.0 1.7 convert_multiply_fusion
  78.7 1.5 fusion.7
  80.2 0.0 all-reduce.4.cloned.1.call-update
  80.3 0.2 all-reduce.6.cloned.1.call-start
  80.5 16.9 %all-reduce.4.cloned.1.call-done = bf16[1,512,512]{2,1,0:T(8,128)(2,1)} async-done(((bf16[1,512,512]{2,1,0:T(8,128)(2,1)}), bf16[1,512,512]{2,1,0:T(8,128)(2,1)}) %all-reduce.4.cloned.1.call-update) | async-done | bytes 524304 | tf_op jit(solution)/shard_map/psum | solution.py:24
  97.4 3.4 %fusion = bf16[512,1024]{1,0:T(8,128)(2,1)} fusion(f32[16,1,32,1024]{3,2,1,0:T(8,128)S(1)} %copy-done, bf16[512,1024]{1,0:T(8,128)(2,1)S(1)} %bitcast.81, bf16[1,512,512]{2,1,0:T(8,128)(2,1)} %all-reduce.4.cloned.1.call-done), kind=kOutput, calls=%fused_computation.5 | convolution fusion | flops 807665664 | bytes 4718592 | tf_op jit(solution)/shard_map/cmk,ckn->cmn/dot_general | solution.py:27
  100.8 3.2 %fusion.8 = bf16[1,512,512]{2,1,0:T(8,128)(2,1)} fusion(bf16[512,1024]{1,0:T(8,128)(2,1)} %fusion), kind=kOutput, calls=%fused_computation.23 | convolution fusion | flops 537133056 | bytes 1572864 | tf_op jit(solution)/shard_map/cmk,cnk->cmn/dot_general | solution.py:33
  104.0 20.1 %all-reduce.6.cloned.1.call-done = bf16[1,512,512]{2,1,0:T(8,128)(2,1)} async-done(((bf16[1,512,512]{2,1,0:T(8,128)(2,1)}), bf16[1,512,512]{2,1,0:T(8,128)(2,1)}) %all-reduce.6.cloned.1.call-update) | async-done | bytes 524304 | tf_op jit(solution)/shard_map/psum | solution.py:24
  124.1 3.2 %multiply_reduce_fusion = (f32[]{:T(128)}, bf16[512,1024]{1,0:T(8,128)(2,1)S(1)}) fusion(bf16[512,1024]{1,0:T(8,128)(2,1)S(1)} %copy-done.6, bf16[1,512,512]{2,1,0:T(8,128)(2,1)} %all-reduce.6.cloned.1.call-done), kind=kOutput, calls=%fused_computation.7 | convolution fusion | flops 810811392 | bytes 2621444 | tf_op jit(solution)/shard_map/cmk,ckn->cmn/dot_general | solution.py:27
  127.3 1.6 copy.18
  128.9 0.5 broadcast.355
  129.5 6.8 %reduce.3 = bf16[512,1024]{1,0:T(8,128)(2,1)S(1)} reduce(bf16[512,1,1,1024]{3,2,1,0:T(2,128)(2,1)S(1)} %bitcast.77, bf16[]{:T(256)} %broadcast.355), dimensions={1,2}, to_apply=%bitcast.75.reduce_sub_computation | reduce | bytes 2097154
  136.3 1.6 reshape.253
  137.9 6.8 %all-to-all-start.1 = ((bf16[16,2,16384]{2,1,0:T(2,128)(2,1)}), bf16[16,2,16384]{2,1,0:T(2,128)(2,1)S(1)}, u32[]{:S(2)}, u32[]{:S(2)}) async-start(bf16[16,2,16384]{2,1,0:T(2,128)(2,1)} %reshape.253), calls=%async_computation.1 | async-start | bytes 2097152 | tf_op jit(solution)/shard_map/all_to_all | solution.py:74
  144.8 0.6 multiply_subtract_fusion
  145.4 3.1 %psum.38 = f32[1]{0:T(128)} all-reduce(f32[1]{0:T(128)} %bitcast.17), channel_id=1, replica_groups=mesh['wide'=16,'narrow'=2] {'narrow'}, use_global_device_ids=true, to_apply=%region_7.8 | all-reduce | flops 1 | bytes 8 | tf_op jit(solution)/shard_map/psum | solution.py:42
  149.2 47.4 %psum.39 = f32[14]{0:T(128)S(1)} all-reduce(f32[14]{0:T(128)S(1)} %compare_select_fusion.5), channel_id=1, replica_groups=mesh['wide'=16,'narrow'=2] {'wide'}, use_global_device_ids=true, to_apply=%region_8.9 | all-reduce | flops 14 | bytes 112 | tf_op jit(solution)/shard_map/psum | solution.py:80
  196.6 0.6 fusion.23
  197.2 1.0 reshape.254
  198.2 0.4 copy.16
  198.6 0.6 gather_fusion.1
  199.2 1.1 broadcast_select_fusion
  (24 shorter events, 0.1 us)
Async XLA Ops:
  7.2 90.2 %all-reduce.4.cloned.1.call-start = ((), (), s32[]{:S(2)}) async-start(), calls=%async_computation.2 | async-start | bytes 1048576 | tf_op jit(solution)/shard_map/psum | solution.py:24
  78.7 18.7 %copy-start = (f32[16,1,32,1024]{3,2,1,0:T(8,128)S(1)}, f32[16,1,32,1024]{3,2,1,0:T(8,128)}, u32[]{:S(2)}) copy-start(f32[16,1,32,1024]{3,2,1,0:T(8,128)} %get-tuple-element.9) | copy-start | bytes 6291460
  80.3 43.8 %all-reduce.6.cloned.1.call-start = ((), (), s32[]{:S(2)}) async-start(), calls=%async_computation.3 | async-start | bytes 1048576 | tf_op jit(solution)/shard_map/psum | solution.py:24
  100.8 23.3 %copy-start.6 = (bf16[512,1024]{1,0:T(8,128)(2,1)S(1)}, bf16[512,1024]{1,0:T(8,128)(2,1)}, u32[]{:S(2)}) copy-start(bf16[512,1024]{1,0:T(8,128)(2,1)} %fusion) | copy-start | bytes 3145732
  136.2 8.5 %copy-start.1 = (f32[14,128]{1,0:T(8,128)S(1)}, f32[14,128]{1,0:T(8,128)}, u32[]{:S(2)}) copy-start(f32[14,128]{1,0:T(8,128)} %param.11) | copy-start | bytes 21508
  136.3 8.5 %copy-start.2 = (f32[14,128]{1,0:T(8,128)S(1)}, f32[14,128]{1,0:T(8,128)}, u32[]{:S(2)}) copy-start(f32[14,128]{1,0:T(8,128)} %param.10) | copy-start | bytes 21508
  136.3 8.5 %copy-start.3 = (f32[14,128]{1,0:T(8,128)S(1)}, f32[14,128]{1,0:T(8,128)}, u32[]{:S(2)}) copy-start(f32[14,128]{1,0:T(8,128)} %param.12) | copy-start | bytes 21508
  136.3 8.5 %copy-start.4 = (f32[14,128]{1,0:T(8,128)S(1)}, f32[14,128]{1,0:T(8,128)}, u32[]{:S(2)}) copy-start(f32[14,128]{1,0:T(8,128)} %param.13) | copy-start | bytes 21508
  136.3 60.3 %copy-start.5 = (s32[14]{0:T(128)S(1)}, s32[14]{0:T(128)}, u32[]{:S(2)}) copy-start(s32[14]{0:T(128)} %param.9) | copy-start | bytes 172
  137.9 59.3 %all-to-all-start.1 = ((bf16[16,2,16384]{2,1,0:T(2,128)(2,1)}), bf16[16,2,16384]{2,1,0:T(2,128)(2,1)S(1)}, u32[]{:S(2)}, u32[]{:S(2)}) async-start(bf16[16,2,16384]{2,1,0:T(2,128)(2,1)} %reshape.253), calls=%async_computation.1 | async-start | bytes 2097152 | tf_op jit(solution)/shard_map/all_to_all | solution.py:74
Sparse Core Ops, SparseCore 0:
  80.4 16.9 all-reduce.3
  104.1 19.9 all-reduce.5
where the time goes:
time: 208 us; the launch traced here: 207 us
  blocking collectives  111 us (53%)
  waiting for transfers between devices  37 us (18%)
  other arithmetic  17.5 us (8%)
  between operations  15.6 us (8%)
  matrix products  11.3 us (5%)
  local copies, waits for them, and re-layouts  8.1 us (4%)
  starting transfers between devices  7.05 us (3%)
    all_to_all x1, blocking collectives, on_device(): lax.all_to_all(outgoing, 'wide', split_axis=0, concat_axis=2, tiled=True)  57 us
    psum x1, blocking collectives, on_device(): matrix_loads = lax.psum(local_loads, 'wide')  47.4 us
    psum x2, waiting for transfers between devices, polynomial_times(): gram_sum = lax.psum(partial_value.astype(jnp.bfloat16), 'narrow')  37 us
    all_to_all x1, starting transfers between devices, on_device(): lax.all_to_all(updates, 'wide', split_axis=2, concat_axis=0, tiled=True)  6.79 us
    unnamed x1, other arithmetic  6.78 us
    dot_general x2, matrix products, polynomial_times(): jnp.einsum('cmk,ckn->cmn', polynomial, current, preferred_element_type=jn...  6.64 us
    dot_general x2, matrix products, newton_schulz(): jnp.einsum('cmk,cnk->cmn', current, current, preferred_element_type=jnp.f...  4.71 us
  transfers between devices with their start and end apart: 3, of which 2 were waited for; matrix products, arithmetic and copies ran while one was open for 1% of the time, Pallas kernels for 0%

commit v1 on v0

--- a/solution.py
+++ b/solution.py
@@ -71,7 +71,10 @@
     updates, slot_loads = orthogonalize(
         lax.all_to_all(outgoing, "wide", split_axis=0, concat_axis=2, tiled=True)
     )
-    returned = lax.all_to_all(updates, "wide", split_axis=2, concat_axis=0, tiled=True)
+    returned = jnp.concatenate(
+        lax.all_to_all(jnp.stack(jnp.split(updates, lax.axis_size("wide"), axis=2)), "wide", 0, 0),
+        axis=0,
+    )
     arrived = returned.reshape(slot_total, row_count, col_count)
     muon_update = jnp.take(arrived, slot_of, axis=0)
     own_group = lax.axis_index("wide")

time: 208 us -> 206 us (level)
  other arithmetic: 17.5 us -> 10.7 us
  local copies, waits for them, and re-layouts: 8.1 us -> 12.9 us
    unnamed x1 -> x0, other arithmetic: 6.78 us -> none
    unnamed x18 -> x29, local copies, waits for them, and re-layouts: 3.57 us -> 9.37 us
where the time goes in v1:
time: 206 us; the launch traced here: 205 us
  blocking collectives  111 us (54%)
  waiting for transfers between devices  37.2 us (18%)
  between operations  15.5 us (8%)
  local copies, waits for them, and re-layouts  12.9 us (6%)
  matrix products  11.4 us (6%)
  other arithmetic  10.7 us (5%)
  starting transfers between devices  6.87 us (3%)
    all_to_all x1, blocking collectives, on_device(): lax.all_to_all(outgoing, 'wide', split_axis=0, concat_axis=2, tiled=True)  57 us
    psum x1, blocking collectives, on_device(): matrix_loads = lax.psum(local_loads, 'wide')  47.4 us
    psum x2, waiting for transfers between devices, polynomial_times(): gram_sum = lax.psum(partial_value.astype(jnp.bfloat16), 'narrow')  37.2 us
    unnamed x29, local copies, waits for them, and re-layouts  9.37 us
    all_to_all x1, starting transfers between devices, on_device(): lax.all_to_all(jnp.stack(jnp.split(updates, lax.axis_size('wide'), axis=2...  6.79 us
    dot_general x2, matrix products, polynomial_times(): jnp.einsum('cmk,ckn->cmn', polynomial, current, preferred_element_type=jn...  6.71 us
    dot_general x2, matrix products, newton_schulz(): jnp.einsum('cmk,cnk->cmn', current, current, preferred_element_type=jnp.f...  4.7 us
  transfers between devices with their start and end apart: 3, of which 2 were waited for; matrix products, arithmetic and copies ran while one was open for 1% of the time, Pallas kernels for 0%

profile of v1, /device:TPU:0, one launch (start us, length us, event | category | flops | bytes accessed | tf_op | source)
XLA Modules:
  0.0 205.2 jit_solution(14227385031190158238)
XLA Ops:
  7.5 3.5 %convert_add_fusion = (f32[14,32,1024]{2,1,0:T(8,128)S(1)}, f32[14,32,1024]{2,1,0:T(8,128)}) fusion(bf16[14,32,1024]{2,1,0:T(8,128)(2,1)} %param.7, f32[14,32,1024]{2,1,0:T(8,128)} %param.8), kind=kLoop, calls=%fused_computation.2 | loop fusion | flops 2293760 | bytes 6422528 | tf_op jit(solution)/shard_map/add | solution.py:56
  11.2 2.0 gather_fusion
  13.3 1.8 bitcast_select_fusion
  15.1 57.0 %all_to_all.14 = f32[16,1,32,1024]{3,2,1,0:T(8,128)S(1)} all-to-all(f32[16,1,32,1024]{3,2,1,0:T(8,128)S(1)} %bitcast_select_fusion), channel_id=1, replica_groups=mesh['wide'=16,'narrow'=2] {'wide'}, dimensions={0} | all-to-all | bytes 4194304 | tf_op jit(solution)/shard_map/all_to_all | solution.py:72
  72.1 1.1 multiply_reduce_fusion.1
  73.2 3.1 %psum.35 = f32[1]{0:T(128)} all-reduce(f32[1]{0:T(128)} %bitcast.3), channel_id=1, replica_groups=mesh['wide'=16,'narrow'=2] {'narrow'}, use_global_device_ids=true, to_apply=%region_3.4 | all-reduce | flops 1 | bytes 8 | tf_op jit(solution)/shard_map/psum | solution.py:48
  77.0 1.7 convert_multiply_fusion
  78.7 1.5 fusion.7
  80.3 17.1 %all-reduce.4.cloned.1.call-done = bf16[1,512,512]{2,1,0:T(8,128)(2,1)} async-done(((bf16[1,512,512]{2,1,0:T(8,128)(2,1)}), bf16[1,512,512]{2,1,0:T(8,128)(2,1)}) %all-reduce.4.cloned.1.call-update) | async-done | bytes 524304 | tf_op jit(solution)/shard_map/psum | solution.py:24
  97.4 3.4 %fusion = bf16[512,1024]{1,0:T(8,128)(2,1)} fusion(f32[16,1,32,1024]{3,2,1,0:T(8,128)S(1)} %copy-done, bf16[512,1024]{1,0:T(8,128)(2,1)S(1)} %bitcast.154, bf16[1,512,512]{2,1,0:T(8,128)(2,1)} %all-reduce.4.cloned.1.call-done), kind=kOutput, calls=%fused_computation.5 | convolution fusion | flops 807665664 | bytes 4718592 | tf_op jit(solution)/shard_map/cmk,ckn->cmn/dot_general | solution.py:27
  100.8 3.2 %fusion.8 = bf16[1,512,512]{2,1,0:T(8,128)(2,1)} fusion(bf16[512,1024]{1,0:T(8,128)(2,1)} %fusion), kind=kOutput, calls=%fused_computation.23 | convolution fusion | flops 537133056 | bytes 1572864 | tf_op jit(solution)/shard_map/cmk,cnk->cmn/dot_general | solution.py:33
  104.0 20.1 %all-reduce.6.cloned.1.call-done = bf16[1,512,512]{2,1,0:T(8,128)(2,1)} async-done(((bf16[1,512,512]{2,1,0:T(8,128)(2,1)}), bf16[1,512,512]{2,1,0:T(8,128)(2,1)}) %all-reduce.6.cloned.1.call-update) | async-done | bytes 524304 | tf_op jit(solution)/shard_map/psum | solution.py:24
  124.1 3.3 %multiply_reduce_fusion = (f32[]{:T(128)}, bf16[512,1024]{1,0:T(8,128)(2,1)S(1)}) fusion(bf16[512,1024]{1,0:T(8,128)(2,1)S(1)} %copy-done.6, bf16[1,512,512]{2,1,0:T(8,128)(2,1)} %all-reduce.6.cloned.1.call-done), kind=kOutput, calls=%fused_computation.7 | convolution fusion | flops 810811392 | bytes 2621444 | tf_op jit(solution)/shard_map/cmk,ckn->cmn/dot_general | solution.py:27
  127.4 0.6 fusion.34
  128.0 0.6 fusion.33
  128.6 0.6 fusion.32
  129.3 0.6 fusion.31
  129.9 0.6 fusion.30
  130.5 0.6 fusion.29
  131.1 0.6 fusion.28
  131.8 0.6 fusion.27
  132.4 0.6 fusion.26
  133.0 0.6 fusion.25
  133.6 0.6 fusion.24
  135.5 0.6 fusion.21
  136.1 0.6 fusion.20
  136.7 0.6 fusion.19
  137.4 6.8 %all-to-all-start.1 = ((bf16[16,1,1,32,1024]{4,3,2,1,0:T(8,128)(2,1)}), bf16[16,1,1,32,1024]{4,3,2,1,0:T(8,128)(2,1)S(1)}, u32[]{:S(2)}, u32[]{:S(2)}) async-start(bf16[16,1,1,32,1024]{4,3,2,1,0:T(8,128)(2,1)} %fusion.19), calls=%async_computation.1 | async-start | bytes 2097152 | tf_op jit(solution)/shard_map/all_to_all | solution.py:75
  144.3 0.6 multiply_subtract_fusion
  144.9 3.1 %psum.38 = f32[1]{0:T(128)} all-reduce(f32[1]{0:T(128)} %bitcast.34), channel_id=1, replica_groups=mesh['wide'=16,'narrow'=2] {'narrow'}, use_global_device_ids=true, to_apply=%region_7.8 | all-reduce | flops 1 | bytes 8 | tf_op jit(solution)/shard_map/psum | solution.py:42
  148.6 47.4 %psum.39 = f32[14]{0:T(128)S(1)} all-reduce(f32[14]{0:T(128)S(1)} %compare_select_fusion.5), channel_id=1, replica_groups=mesh['wide'=16,'narrow'=2] {'wide'}, use_global_device_ids=true, to_apply=%region_8.9 | all-reduce | flops 14 | bytes 112 | tf_op jit(solution)/shard_map/psum | solution.py:83
  197.3 1.1 broadcast_select_fusion
  (34 shorter events, 3.1 us)
Async XLA Ops:
  7.2 90.2 %all-reduce.4.cloned.1.call-start = ((), (), s32[]{:S(2)}) async-start(), calls=%async_computation.2 | async-start | bytes 1048576 | tf_op jit(solution)/shard_map/psum | solution.py:24
  78.7 18.7 %copy-start = (f32[16,1,32,1024]{3,2,1,0:T(8,128)S(1)}, f32[16,1,32,1024]{3,2,1,0:T(8,128)}, u32[]{:S(2)}) copy-start(f32[16,1,32,1024]{3,2,1,0:T(8,128)} %get-tuple-element.9) | copy-start | bytes 6291460
  80.3 43.8 %all-reduce.6.cloned.1.call-start = ((), (), s32[]{:S(2)}) async-start(), calls=%async_computation.3 | async-start | bytes 1048576 | tf_op jit(solution)/shard_map/psum | solution.py:24
  100.8 23.3 %copy-start.6 = (bf16[512,1024]{1,0:T(8,128)(2,1)S(1)}, bf16[512,1024]{1,0:T(8,128)(2,1)}, u32[]{:S(2)}) copy-start(bf16[512,1024]{1,0:T(8,128)(2,1)} %fusion) | copy-start | bytes 3145732
  127.4 16.8 %copy-start.1 = (f32[14,128]{1,0:T(8,128)S(1)}, f32[14,128]{1,0:T(8,128)}, u32[]{:S(2)}) copy-start(f32[14,128]{1,0:T(8,128)} %param.11) | copy-start | bytes 21508
  127.4 16.9 %copy-start.2 = (f32[14,128]{1,0:T(8,128)S(1)}, f32[14,128]{1,0:T(8,128)}, u32[]{:S(2)}) copy-start(f32[14,128]{1,0:T(8,128)} %param.10) | copy-start | bytes 21508
  127.4 16.9 %copy-start.3 = (f32[14,128]{1,0:T(8,128)S(1)}, f32[14,128]{1,0:T(8,128)}, u32[]{:S(2)}) copy-start(f32[14,128]{1,0:T(8,128)} %param.12) | copy-start | bytes 21508
  127.4 16.9 %copy-start.4 = (f32[14,128]{1,0:T(8,128)S(1)}, f32[14,128]{1,0:T(8,128)}, u32[]{:S(2)}) copy-start(f32[14,128]{1,0:T(8,128)} %param.13) | copy-start | bytes 21508
  128.0 68.0 %copy-start.5 = (s32[14]{0:T(128)S(1)}, s32[14]{0:T(128)}, u32[]{:S(2)}) copy-start(s32[14]{0:T(128)} %param.9) | copy-start | bytes 172
  137.4 59.3 %all-to-all-start.1 = ((bf16[16,1,1,32,1024]{4,3,2,1,0:T(8,128)(2,1)}), bf16[16,1,1,32,1024]{4,3,2,1,0:T(8,128)(2,1)S(1)}, u32[]{:S(2)}, u32[]{:S(2)}) async-start(bf16[16,1,1,32,1024]{4,3,2,1,0:T(8,128)(2,1)} %fusion.19), calls=%async_computation.1 | async-start | bytes 2097152 | tf_op jit(solution)/shard_map/all_to_all | solution.py:75
Sparse Core Ops, SparseCore 0:
  80.4 16.9 all-reduce.3
  104.1 19.8 all-reduce.5
